TPU v7x, 512 devices: a whole 4x4x16 slice. The times are simulated.
512 devices in a mesh: tm: 16 (over z_lo, y), series: 32 (over z_hi, x, core).
Axes of the slice: x: 4, y: 4, z: 16 (z_hi: 4, z_lo: 4; z = z_hi * 4 + z_lo), core: 2. Of those that a mesh axis runs over, the one named last changes fastest.
Arguments:
- inputs: bfloat16 [64, 8192, 512], P('series', 'tm'), may hold values from -6 to 6
- cotangent: bfloat16 [64, 8192, 512], P('series', 'tm'), may hold values from -6 to 6
- taps: int32 [3], replicated, may hold values from 0 to 128, as said below
- weight: float32 [1536, 512], P('series'), may hold values from -0.15625 to 0.15625
- moment_one: float32 [1536, 512], P('series'), may hold values from -10 to 10
- second_moment_state: float32 [1536, 512], P('series'), may hold values from 1 to 100
Outputs:
- grad_input: bfloat16 [64, 8192, 512], P('series', 'tm')
- new_weight: float32 [1536, 512], P('series')
- new_moment_one: float32 [1536, 512], P('series')
- new_moment_two: float32 [1536, 512], P('series')
Inputs may be any that keep to these rules, and one draw needn't show every extreme that they name: taps[0] is 0, taps[2] is 128, and taps[1] lies strictly between them.
All inputs are finite; a program needn't handle non-finite values.
Results may differ from a plain program's by a relative error of at most 0.0045.
Values may be sent and summed in bfloat16 or wider, within the bound.
No kernel may reach another device: no remote copies, remote signals or barrier semaphores. Data moves between devices by JAX's collectives and lax.ppermute only.
A program may use at most 64 MiB of HBM per device.

v0:
```python
import jax
import jax.numpy as jnp
from jax import lax
from jax.sharding import PartitionSpec as P

DILATION_GAP = 64


def passed_along(array, axis, by):
    size = lax.axis_size(axis)
    pairs = [(i, i + by) for i in range(size) if 0 <= i + by < size]
    return lax.ppermute(array, axis, pairs)


def adamw(weight, grad, moment_one, second_moment_state):
    first = 0.9 * moment_one + 0.1 * grad
    second = 0.999 * second_moment_state + 0.001 * grad * grad
    unbiased_one = first / (1.0 - 0.9**10)
    unbiased_two = second / (1.0 - 0.999**10)
    updated = weight - 0.01 * (unbiased_one / (jnp.sqrt(unbiased_two) + 1e-08) + 0.1 * weight)
    return (updated, first, second)


def body(inputs, cotangent, taps, weight, moment_one, second_moment_state):
    series_n, time_n, width = inputs.shape
    tap_count = taps.shape[0]
    receptive_span = (tap_count - 1) * DILATION_GAP
    rows = series_n * time_n
    wide = lax.all_gather(weight.astype(jnp.bfloat16), "series", axis=0, tiled=True)
    earlier = passed_along(inputs[:, time_n - receptive_span :, :], "tm", 1)
    extended = jnp.concatenate([earlier, inputs], 1)
    shifted = [
        lax.dynamic_slice_in_dim(extended, receptive_span - taps[k], time_n, 1)
        for k in range(tap_count)
    ]
    stacked = jnp.concatenate(shifted, 2).reshape(rows, tap_count * width)
    pre = jnp.dot(stacked, wide, preferred_element_type=jnp.float32)
    sig = jax.nn.sigmoid(pre)
    upstream = cotangent.reshape(rows, width)
    dpre_flat = (upstream.astype(jnp.float32) * (sig * (1.0 + pre * (1.0 - sig)))).astype(
        jnp.bfloat16
    )
    dpre = dpre_flat.reshape(series_n, time_n, width)
    ahead = passed_along(dpre[:, :receptive_span, :], "tm", -1)
    later = jnp.concatenate([dpre, ahead], 1)
    result = upstream.astype(jnp.float32)
    for k in range(tap_count):
        moved = lax.dynamic_slice_in_dim(later, taps[k], time_n, 1).reshape(rows, width)
        result = result + lax.dot_general(
            moved,
            wide[k * width : (k + 1) * width],
            (((1,), (1,)), ((), ())),
            preferred_element_type=jnp.float32,
        )
    grad_input = result.astype(jnp.bfloat16).reshape(series_n, time_n, width)
    grad_shard = lax.psum_scatter(
        lax.dot_general(
            stacked, dpre_flat, (((0,), (0,)), ((), ())), preferred_element_type=jnp.float32
        ),
        "series",
        scatter_dimension=0,
        tiled=True,
    )
    grad_shard = lax.psum(grad_shard, "tm")
    new_weight, new_moment_one, new_moment_two = adamw(
        weight, grad_shard, moment_one, second_moment_state
    )
    return (grad_input, new_weight, new_moment_one, new_moment_two)


def solution(mesh):
    in_specs = (
        P("series", "tm", None),
        P("series", "tm", None),
        P(),
        P("series", None),
        P("series", None),
        P("series", None),
    )
    out_specs = (P("series", "tm", None), P("series", None), P("series", None), P("series", None))
    return jax.shard_map(body, mesh=mesh, in_specs=in_specs, out_specs=out_specs, check_vma=False)
```

profile of v0, /device:TPU:2, one launch (start us, length us, event | category | flops | bytes accessed | tf_op | source)
XLA Modules:
  0.0 394.1 jit_solution(17457735593663713182)
XLA Ops:
  7.2 0.0 all-gather.2.cloned.1.call-start
  7.2 1.5 convert_element_type.18
  8.7 0.0 all-gather.2.cloned.1.call-update
  8.8 0.0 reduce-scatter.2.cloned.1.call-start
  8.8 1.0 slice.27
  9.8 3.5 collective-permute-start
  13.3 1.4 fusion.14
  18.4 0.5 collective-permute-done
  18.8 1.3 constant_dynamic-update-slice_fusion
  20.1 0.8 constant_dynamic-slice_fusion.2
  20.9 0.3 pad_maximum_fusion
  21.2 69.6 %all-gather.2.cloned.1.call-done = bf16[1536,512]{1,0:T(8,128)(2,1)} async-done(((bf16[48,512]{1,0:T(8,128)(2,1)}), bf16[1536,512]{1,0:T(8,128)(2,1)}) %all-gather.2.cloned.1.call-update) | async-done | bytes 1572880 | tf_op jit(solution)/shard_map/all_gather | solution.py:29
  90.8 4.0 %fusion = bf16[1024,512]{1,0:T(8,128)(2,1)S(1)} fusion(bf16[2,512,512]{2,1,0:T(8,128)(2,1)} %param.7, bf16[1024,1536]{1,0:T(8,128)(2,1)S(1)} %bitcast.22, bf16[1536,512]{1,0:T(8,128)(2,1)} %all-gather.2.cloned.1.call-done), kind=kOutput, calls=%fused_computation.3 | convolution fusion | flops 1615855616 | bytes 6815744 | tf_op jit(solution)/shard_map/dot_general | solution.py:37
  94.8 0.0 copy-start
  94.8 1.0 copy-done
  95.8 3.5 fusion.15
  99.3 0.0 reduce-scatter.2.cloned.1.call-update
  99.3 0.0 all-reduce.2.cloned.1.call-start
  99.3 1.1 copy-done.1
  100.5 1.3 collective-permute-start.1
  107.4 5.1 %collective-permute-done.1 = bf16[2,128,512]{2,1,0:T(8,128)(2,1)S(1)} collective-permute-done((bf16[2,128,512]{2,1,0:T(8,128)(2,1)S(1)}, bf16[2,128,512]{2,1,0:T(8,128)(2,1)S(1)}, u32[]{:S(2)}, u32[]{:S(2)}) %collective-permute-start.1) | collective-permute-done | bytes 262176 | tf_op jit(solution)/shard_map/ppermute | solution.py:12
  112.5 3.1 fusion.4
  115.6 0.7 fusion.10
  116.3 2.1 fusion.8
  118.4 106.4 %reduce-scatter.2.cloned.1.call-done = f32[48,512]{1,0:T(8,128)} async-done(((f32[1536,512]{1,0:T(8,128)}), f32[48,512]{1,0:T(8,128)}) %reduce-scatter.2.cloned.1.call-update) | async-done | bytes 98320 | tf_op jit(solution)/shard_map/reduce_scatter | solution.py:56
  224.8 0.0 all-reduce.2.cloned.1.call-update
  224.8 0.0 copy-start.3
  224.8 0.0 copy-start.4
  224.8 0.0 copy-start.5
  224.9 3.8 fusion.3
  228.7 157.2 %all-reduce.2.cloned.1.call-done = f32[48,512]{1,0:T(8,128)} async-done(((f32[48,512]{1,0:T(8,128)}), f32[48,512]{1,0:T(8,128)}) %all-reduce.2.cloned.1.call-update) | async-done | bytes 98320 | tf_op jit(solution)/shard_map/psum | solution.py:64
  385.9 1.6 multiply_subtract_fusion
  (8 shorter events, 0.0 us)
Async XLA Ops:
  7.2 83.6 %all-gather.2.cloned.1.call-start = ((), (), s32[]{:S(2)}) async-start(), calls=%async_computation.1 | async-start | bytes 1622016 | tf_op jit(solution)/shard_map/all_gather | solution.py:29
  8.8 216.0 %reduce-scatter.2.cloned.1.call-start = ((), (), s32[]{:S(2)}) async-start(), calls=%async_computation.2 | async-start | bytes 3244032 | tf_op jit(solution)/shard_map/reduce_scatter | solution.py:56
  9.8 9.0 %collective-permute-start = (bf16[2,128,512]{2,1,0:T(8,128)(2,1)S(1)}, bf16[2,128,512]{2,1,0:T(8,128)(2,1)S(1)}, u32[]{:S(2)}, u32[]{:S(2)}) collective-permute-start(bf16[2,128,512]{2,1,0:T(8,128)(2,1)S(1)} %slice.27), channel_id=1, source_target_pairs={{0,32},{32,64},{64,96},{96,128},{128,160},{160,192},{192,224},{224... | collective-permute-start | bytes 786440 | tf_op jit(solution)/shard_map/ppermute | solution.py:12
  94.8 1.0 copy-start
  99.3 1.2 copy-start.1
  99.3 286.6 %all-reduce.2.cloned.1.call-start = ((), (), s32[]{:S(2)}) async-start(), calls=%async_computation.3 | async-start | bytes 196608 | tf_op jit(solution)/shard_map/psum | solution.py:64
  100.5 12.0 %collective-permute-start.1 = (bf16[2,128,512]{2,1,0:T(8,128)(2,1)S(1)}, bf16[2,128,512]{2,1,0:T(8,128)(2,1)S(1)}, u32[]{:S(2)}, u32[]{:S(2)}) collective-permute-start(bf16[2,128,512]{2,1,0:T(8,128)(2,1)S(1)} %slice.35), channel_id=1, source_target_pairs={{32,0},{64,32},{96,64},{128,96},{160,128},{192,160},{224,192},{256... | collective-permute-start | bytes 786440 | tf_op jit(solution)/shard_map/ppermute | solution.py:12
  107.4 8.2 %copy-start.2 = (bf16[1536,512]{1,0:T(8,128)(2,1)S(1)}, bf16[1536,512]{1,0:T(8,128)(2,1)}, u32[]{:S(2)}) copy-start(bf16[1536,512]{1,0:T(8,128)(2,1)} %all-gather.2.cloned.1.call-done) | copy-start | bytes 4718596
  224.8 161.1 %copy-start.3 = (f32[48,512]{1,0:T(8,128)S(1)}, f32[48,512]{1,0:T(8,128)}, u32[]{:S(2)}) copy-start(f32[48,512]{1,0:T(8,128)} %param.9) | copy-start | bytes 294916
  224.8 161.1 %copy-start.4 = (f32[48,512]{1,0:T(8,128)S(1)}, f32[48,512]{1,0:T(8,128)}, u32[]{:S(2)}) copy-start(f32[48,512]{1,0:T(8,128)} %param.10) | copy-start | bytes 294916
  224.8 161.0 %copy-start.5 = (f32[48,512]{1,0:T(8,128)S(1)}, f32[48,512]{1,0:T(8,128)}, u32[]{:S(2)}) copy-start(f32[48,512]{1,0:T(8,128)} %param.11) | copy-start | bytes 294916
Sparse Core Ops, SparseCore 0:
  11.7 79.0 all-gather.1
  99.4 125.3 reduce-scatter.1
  228.0 157.8 all-reduce.1
where the time goes:
time: 395 us; the launch traced here: 394 us
  waiting for transfers between devices  339 us (86%)
  between operations  23.1 us (6%)
  matrix products  14.2 us (4%)
  local copies, waits for them, and re-layouts  6.59 us (2%)
  other arithmetic  6.47 us (2%)
  starting transfers between devices  4.91 us (1%)
    psum x1, waiting for transfers between devices, body(): grad_shard = lax.psum(grad_shard, 'tm')  157 us
    reduce_scatter x1, waiting for transfers between devices, body(): lax.psum_scatter(lax.dot_general(stacked, dpre_flat, (((0,), (0,)), ((),...  106 us
    all_gather x1, waiting for transfers between devices, body(): lax.all_gather(weight.astype(jnp.bfloat16), 'series', axis=0, tiled=True)  69.6 us
  transfers between devices with their start and end apart: 5, of which 5 were waited for; matrix products, arithmetic and copies ran while one was open for 4% of the time, Pallas kernels for 0%

commit v1 on v0

--- a/solution.py
+++ b/solution.py
@@ -4,6 +4,12 @@
 from jax.sharding import PartitionSpec as P
 
 DILATION_GAP = 64
+
+
+def gather_and_add(x, name):
+    parts = lax.all_gather(x, name, axis=0, tiled=False)
+    total = parts.sum(axis=0)
+    return total
 
 
 def passed_along(array, axis, by):
@@ -61,7 +67,7 @@
         scatter_dimension=0,
         tiled=True,
     )
-    grad_shard = lax.psum(grad_shard, "tm")
+    grad_shard = gather_and_add(grad_shard, "tm")
     new_weight, new_moment_one, new_moment_two = adamw(
         weight, grad_shard, moment_one, second_moment_state
     )

time: 395 us -> 319 us (0.81)
  waiting for transfers between devices: 339 us -> 267 us
    psum x1 -> x0, waiting for transfers between devices: 157 us -> none  [body(): grad_shard = lax.psum(grad_shard, 'tm')]
    all_gather x0 -> x1, waiting for transfers between devices: none -> 69.3 us  [gather_and_add(): parts = lax.all_gather(x, name, axis=0, tiled=False)]
    reduce_scatter x1, waiting for transfers between devices: 106 us -> 125 us  [body(): lax.psum_scatter(lax.dot_general(stacked, dpre_flat, (((0,), (0,)), ((),...]
  transfers between devices with their start and end apart: 5 -> 5, of which waited for: 5 -> 5; matrix products, arithmetic and copies ran while one was open for 4% -> 3% of each run, Pallas kernels for 0% -> 0%
where the time goes in v1:
time: 319 us
  waiting for transfers between devices  267 us (84%)
  between operations  23.5 us (7%)
  matrix products  10.8 us (3%)
  other arithmetic  7.1 us (2%)
  local copies, waits for them, and re-layouts  5.94 us (2%)
  starting transfers between devices  4.91 us (2%)
    reduce_scatter x1, waiting for transfers between devices, body(): lax.psum_scatter(lax.dot_general(stacked, dpre_flat, (((0,), (0,)), ((),...  125 us
    all_gather x1, waiting for transfers between devices, body(): lax.all_gather(weight.astype(jnp.bfloat16), 'series', axis=0, tiled=True)  69.6 us
    all_gather x1, waiting for transfers between devices, gather_and_add(): parts = lax.all_gather(x, name, axis=0, tiled=False)  69.3 us
  transfers between devices with their start and end apart: 5, of which 5 were waited for; matrix products, arithmetic and copies ran while one was open for 3% of the time, Pallas kernels for 0%

profile of v1, /device:TPU:2, one launch (start us, length us, event | category | flops | bytes accessed | tf_op | source)
XLA Modules:
  0.0 319.0 jit_solution(15395463038803049072)
XLA Ops:
  7.2 0.0 all-gather.4.cloned.1.call-start
  7.2 1.5 convert_element_type.18
  8.7 0.0 all-gather.4.cloned.1.call-update
  8.8 0.0 reduce-scatter.2.cloned.1.call-start
  8.8 1.0 slice.27
  9.8 3.5 %collective-permute-start = (bf16[2,128,512]{2,1,0:T(8,128)(2,1)S(1)}, bf16[2,128,512]{2,1,0:T(8,128)(2,1)S(1)}, u32[]{:S(2)}, u32[]{:S(2)}) collective-permute-start(bf16[2,128,512]{2,1,0:T(8,128)(2,1)S(1)} %slice.27), channel_id=1, source_target_pairs={{0,32},{32,64},{64,96},{96,128},{128,160},{160,192},{192,224},{224... | collective-permute-start | bytes 786440 | tf_op jit(solution)/shard_map/ppermute | solution.py:18
  13.3 1.4 fusion.14
  18.5 0.3 collective-permute-done
  18.8 1.3 constant_dynamic-update-slice_fusion
  20.1 0.8 constant_dynamic-slice_fusion.2
  20.9 0.3 pad_maximum_fusion
  21.2 69.6 %all-gather.4.cloned.1.call-done = bf16[1536,512]{1,0:T(8,128)(2,1)} async-done(((bf16[48,512]{1,0:T(8,128)(2,1)}), bf16[1536,512]{1,0:T(8,128)(2,1)}) %all-gather.4.cloned.1.call-update) | async-done | bytes 1572880 | tf_op jit(solution)/shard_map/all_gather | solution.py:35
  90.8 4.0 %fusion = bf16[1024,512]{1,0:T(8,128)(2,1)S(1)} fusion(bf16[2,512,512]{2,1,0:T(8,128)(2,1)} %param.7, bf16[1024,1536]{1,0:T(8,128)(2,1)S(1)} %bitcast.23, bf16[1536,512]{1,0:T(8,128)(2,1)} %all-gather.4.cloned.1.call-done), kind=kOutput, calls=%fused_computation.3 | convolution fusion | flops 1615855616 | bytes 6815744 | tf_op jit(solution)/shard_map/dot_general | solution.py:43
  94.8 0.0 copy-start
  94.8 1.0 copy-done
  95.8 3.5 %fusion.15 = f32[1536,512]{1,0:T(8,128)} fusion(bf16[1024,1536]{1,0:T(8,128)(2,1)S(1)} %bitcast.24, bf16[1024,512]{1,0:T(8,128)(2,1)S(1)} %fusion), kind=kOutput, calls=%fused_computation.31 | convolution fusion | flops 1610612736 | bytes 7340032 | tf_op jit(solution)/shard_map/dot_general | solution.py:63
  99.3 0.0 reduce-scatter.2.cloned.1.call-update
  99.3 0.0 all-gather.6.cloned.1.call-start
  99.4 125.5 %reduce-scatter.2.cloned.1.call-done = f32[48,512]{1,0:T(8,128)} async-done(((f32[1536,512]{1,0:T(8,128)}), f32[48,512]{1,0:T(8,128)}) %reduce-scatter.2.cloned.1.call-update) | async-done | bytes 98320 | tf_op jit(solution)/shard_map/reduce_scatter | solution.py:62
  224.8 0.0 all-gather.6.cloned.1.call-update
  224.9 1.3 collective-permute-start.1
  232.0 0.0 copy-start.2
  232.0 2.0 collective-permute-done.1
  234.0 3.1 fusion.4
  237.1 0.7 fusion.10
  237.8 0.0 copy-start.3
  237.8 0.7 fusion.8
  238.6 0.5 copy-done.3
  239.0 1.8 fusion.3
  240.8 69.3 %all-gather.6.cloned.1.call-done = f32[768,512]{1,0:T(8,128)} async-done(((f32[48,512]{1,0:T(8,128)}), f32[768,512]{1,0:T(8,128)}) %all-gather.6.cloned.1.call-update) | async-done | bytes 1572880 | tf_op jit(solution)/shard_map/all_gather | solution.py:10
  310.2 1.5 reduce_sum.9
  311.7 0.7 multiply_subtract_fusion
  (11 shorter events, 0.1 us)
Async XLA Ops:
  7.2 83.6 %all-gather.4.cloned.1.call-start = ((), (), s32[]{:S(2)}) async-start(), calls=%async_computation.1 | async-start | bytes 1622016 | tf_op jit(solution)/shard_map/all_gather | solution.py:35
  8.8 216.1 %reduce-scatter.2.cloned.1.call-start = ((), (), s32[]{:S(2)}) async-start(), calls=%async_computation.2 | async-start | bytes 3244032 | tf_op jit(solution)/shard_map/reduce_scatter | solution.py:62
  9.8 9.0 %collective-permute-start = (bf16[2,128,512]{2,1,0:T(8,128)(2,1)S(1)}, bf16[2,128,512]{2,1,0:T(8,128)(2,1)S(1)}, u32[]{:S(2)}, u32[]{:S(2)}) collective-permute-start(bf16[2,128,512]{2,1,0:T(8,128)(2,1)S(1)} %slice.27), channel_id=1, source_target_pairs={{0,32},{32,64},{64,96},{96,128},{128,160},{160,192},{192,224},{224... | collective-permute-start | bytes 786440 | tf_op jit(solution)/shard_map/ppermute | solution.py:18
  94.8 1.0 copy-start
  99.3 125.6 %copy-start.1 = (bf16[1024,512]{1,0:T(8,128)(2,1)S(1)}, bf16[1024,512]{1,0:T(8,128)(2,1)}, u32[]{:S(2)}) copy-start(bf16[1024,512]{1,0:T(8,128)(2,1)} %copy-done) | copy-start | bytes 3145732
  99.3 210.9 %all-gather.6.cloned.1.call-start = ((), (), s32[]{:S(2)}) async-start(), calls=%async_computation.3 | async-start | bytes 1671168 | tf_op jit(solution)/shard_map/all_gather | solution.py:10
  224.9 9.1 %collective-permute-start.1 = (bf16[2,128,512]{2,1,0:T(8,128)(2,1)S(1)}, bf16[2,128,512]{2,1,0:T(8,128)(2,1)S(1)}, u32[]{:S(2)}, u32[]{:S(2)}) collective-permute-start(bf16[2,128,512]{2,1,0:T(8,128)(2,1)S(1)} %slice.35), channel_id=1, source_target_pairs={{32,0},{64,32},{96,64},{128,96},{160,128},{192,160},{224,192},{256... | collective-permute-start | bytes 786440 | tf_op jit(solution)/shard_map/ppermute | solution.py:18
  232.0 5.1 %copy-start.2 = (bf16[1536,512]{1,0:T(8,128)(2,1)S(1)}, bf16[1536,512]{1,0:T(8,128)(2,1)}, u32[]{:S(2)}) copy-start(bf16[1536,512]{1,0:T(8,128)(2,1)} %all-gather.4.cloned.1.call-done) | copy-start | bytes 4718596
  237.8 1.2 copy-start.3
  239.0 72.6 %copy-start.4 = (f32[48,512]{1,0:T(8,128)S(1)}, f32[48,512]{1,0:T(8,128)}, u32[]{:S(2)}) copy-start(f32[48,512]{1,0:T(8,128)} %param.9) | copy-start | bytes 294916
  239.0 72.7 %copy-start.5 = (f32[48,512]{1,0:T(8,128)S(1)}, f32[48,512]{1,0:T(8,128)}, u32[]{:S(2)}) copy-start(f32[48,512]{1,0:T(8,128)} %param.10) | copy-start | bytes 294916
  239.0 72.7 %copy-start.6 = (f32[48,512]{1,0:T(8,128)S(1)}, f32[48,512]{1,0:T(8,128)}, u32[]{:S(2)}) copy-start(f32[48,512]{1,0:T(8,128)} %param.11) | copy-start | bytes 294916
Sparse Core Ops, SparseCore 0:
  11.7 79.0 all-gather.3
  99.4 125.3 reduce-scatter.1
  227.1 83.0 all-gather.5
